TPU v7x, 256 devices: a whole 4x4x8 slice. The times are simulated.
256 devices in a mesh: section: 32 (over x_hi, z, core), expert: 8 (over x_lo, y).
Axes of the slice: x: 4 (x_hi: 2, x_lo: 2; x = x_hi * 2 + x_lo), y: 4, z: 8, core: 2. Of those that a mesh axis runs over, the one named last changes fastest.
Arguments:
- tokens: bfloat16 [1536, 6144], P('expert', 'section'), may hold values from -6 to 6
- expert_ids: int32 [1536, 2], P('expert'), may hold values from 0 to 7, as said below
- slot_ids: int32 [1536, 2], P('expert'), may hold values from 0 to 47, as said below
- router: float32 [6144, 8], replicated, may hold values from -0.078125 to 0.078125
- up_weight: bfloat16 [8, 6144, 8192], P('expert', None, 'section'), may hold values from -0.078125 to 0.078125
- down_weight: bfloat16 [8, 8192, 6144], P('expert', 'section'), may hold values from -0.0625 to 0.0625
- cotangent: bfloat16 [1536, 6144], P('expert', 'section'), may hold values from -6 to 6
Outputs:
- mixed: bfloat16 [1536, 6144], P('expert', 'section')
- grad_tokens: bfloat16 [1536, 6144], P('expert', 'section')
- grad_up: bfloat16 [8, 6144, 8192], P('expert', None, 'section')
- grad_down: bfloat16 [8, 8192, 6144], P('expert', 'section')
- grad_router: float32 [6144, 8], replicated
Inputs may be any that keep to these rules, and one draw needn't show every extreme that they name: `expert_ids`: within each block of 192 consecutive tokens (one group), a token's two experts differ and every expert is chosen exactly 48 times. `slot_ids`: within each block of 192 consecutive tokens, the 48 choices of one expert take the slots 0 to 47 once each.
All inputs are finite; a program needn't handle non-finite values.
Results may differ from a plain program's by a relative error of at most 0.019.
Values may be sent and summed in bfloat16 or wider, within the bound.
A program may use at most 128 MiB of HBM per device.

v0:
```python
import jax
import jax.numpy as jnp
from jax import lax
from jax.sharding import PartitionSpec as P


def gate_values(logits, choose):
    picked = jnp.sum(logits[:, None, :] * choose, axis=2)
    logit_gap = picked[:, 0] - picked[:, 1]
    return jnp.stack([jax.nn.sigmoid(logit_gap), jax.nn.sigmoid(-logit_gap)], axis=1)


def dispatch_rows(slot_place, gate_pair, rows_in, rows_cot, slot_total):
    select = (
        jnp.arange(slot_total, dtype=jnp.int32)[:, None, None] == slot_place[None, :, :]
    ).astype(jnp.float32)
    gate_row = jnp.sum(select * gate_pair[None, :, :], axis=(1, 2))
    picker = jnp.sum(select, axis=2).astype(jnp.bfloat16)
    sent_in = jnp.dot(picker, rows_in, preferred_element_type=jnp.float32).astype(jnp.bfloat16)
    sent_cot = jnp.dot(picker, rows_cot, preferred_element_type=jnp.float32)
    sent_cot = (sent_cot * gate_row[:, None]).astype(jnp.bfloat16)
    return (sent_in, sent_cot)


def shards(tokens, expert_ids, slot_ids, router, up_weight, down_weight, cotangent):
    token_count, feat_slice = tokens.shape
    model_width, n_expert = router.shape
    slot_cap = 2 * token_count // n_expert
    slot_total = n_expert * slot_cap
    feat_start = lax.axis_index("section") * feat_slice
    router_rows = lax.dynamic_slice_in_dim(router, feat_start, feat_slice, 0)
    choose = (
        expert_ids[:, :, None] == jnp.arange(n_expert, dtype=jnp.int32)[None, None, :]
    ).astype(jnp.float32)
    slot_place = expert_ids * slot_cap + slot_ids
    full_in, full_cot = (
        lax.all_gather(tokens, "section", axis=1, tiled=True),
        lax.all_gather(cotangent, "section", axis=1, tiled=True),
    )
    logits = jnp.dot(full_in.astype(jnp.float32), router, precision=lax.Precision.HIGHEST)
    gate_pair = gate_values(logits, choose)
    sent_in, sent_cot = dispatch_rows(slot_place, gate_pair, full_in, full_cot, slot_total)
    block_shape = (n_expert, slot_cap, model_width)
    rows_in, rows_cot = (
        lax.all_to_all(
            sent_in.reshape(block_shape), "expert", split_axis=0, concat_axis=0, tiled=True
        ),
        lax.all_to_all(
            sent_cot.reshape(block_shape), "expert", split_axis=0, concat_axis=0, tiled=True
        ),
    )
    rows_in = rows_in.reshape(slot_total, model_width)
    rows_cot = rows_cot.reshape(slot_total, model_width)
    weight_in = up_weight[0]
    weight_out = down_weight[0]
    pre_act = jnp.dot(rows_in, weight_in, preferred_element_type=jnp.float32)
    sigma = jax.nn.sigmoid(pre_act)
    hidden = (pre_act * sigma).astype(jnp.bfloat16)
    hidden_grad = lax.dot_general(
        rows_cot, weight_out, (((1,), (1,)), ((), ())), preferred_element_type=jnp.float32
    )
    pre_grad = (hidden_grad * sigma * (1.0 + pre_act * (1.0 - sigma))).astype(jnp.bfloat16)
    grad_down = lax.dot_general(
        hidden, rows_cot, (((0,), (0,)), ((), ())), preferred_element_type=jnp.float32
    ).astype(jnp.bfloat16)
    grad_up = lax.dot_general(
        rows_in, pre_grad, (((0,), (0,)), ((), ())), preferred_element_type=jnp.float32
    ).astype(jnp.bfloat16)
    forward_part = jnp.dot(hidden, weight_out, preferred_element_type=jnp.float32)
    backward_part = lax.dot_general(
        pre_grad, weight_in, (((1,), (1,)), ((), ())), preferred_element_type=jnp.float32
    )
    out_sum, back_sum = (
        lax.psum_scatter(
            forward_part.astype(jnp.bfloat16), "section", scatter_dimension=1, tiled=True
        ).astype(jnp.float32),
        lax.psum_scatter(
            backward_part.astype(jnp.bfloat16), "section", scatter_dimension=1, tiled=True
        ).astype(jnp.float32),
    )
    return_shape = (n_expert, slot_cap, feat_slice)
    came_out, came_back = (
        lax.all_to_all(
            out_sum.astype(jnp.bfloat16).reshape(return_shape),
            "expert",
            split_axis=0,
            concat_axis=0,
            tiled=True,
        ),
        lax.all_to_all(
            back_sum.astype(jnp.bfloat16).reshape(return_shape),
            "expert",
            split_axis=0,
            concat_axis=0,
            tiled=True,
        ),
    )
    flat_out = came_out.reshape(slot_total, feat_slice)
    flat_back = came_back.reshape(slot_total, feat_slice)
    positions = jnp.arange(slot_total, dtype=jnp.int32)
    take_first = (slot_place[:, 0:1] == positions[None, :]).astype(jnp.bfloat16)
    take_second = (slot_place[:, 1:2] == positions[None, :]).astype(jnp.bfloat16)
    out_first = jnp.dot(take_first, flat_out, preferred_element_type=jnp.float32)
    out_second = jnp.dot(take_second, flat_out, preferred_element_type=jnp.float32)
    mixed = gate_pair[:, 0:1] * out_first + gate_pair[:, 1:2] * out_second
    cot_float = cotangent.astype(jnp.float32)
    grad_first, grad_second = lax.psum(
        (jnp.sum(cot_float * out_first, axis=1), jnp.sum(cot_float * out_second, axis=1)), "section"
    )
    logit_grad = (grad_first - grad_second) * gate_pair[:, 0] * gate_pair[:, 1]
    logits_grad = (choose[:, 0, :] - choose[:, 1, :]) * logit_grad[:, None]
    back_first = jnp.dot(take_first, flat_back, preferred_element_type=jnp.float32)
    back_second = jnp.dot(take_second, flat_back, preferred_element_type=jnp.float32)
    grad_tokens = (
        back_first
        + back_second
        + jnp.dot(logits_grad, router_rows.T, precision=lax.Precision.HIGHEST)
    )
    local_router = jnp.dot(
        tokens.astype(jnp.float32).T, logits_grad, precision=lax.Precision.HIGHEST
    )
    placed_router = lax.dynamic_update_slice(
        jnp.zeros((model_width, n_expert), jnp.float32), local_router, (feat_start, jnp.int32(0))
    )
    grad_router = lax.psum(placed_router, ("section", "expert"))
    return (
        mixed.astype(jnp.bfloat16),
        grad_tokens.astype(jnp.bfloat16),
        grad_up[None],
        grad_down[None],
        grad_router,
    )


def solution(mesh):
    in_specs = (
        P("expert", "section"),
        P("expert", None),
        P("expert", None),
        P(),
        P("expert", None, "section"),
        P("expert", "section", None),
        P("expert", "section"),
    )
    out_specs = (
        P("expert", "section"),
        P("expert", "section"),
        P("expert", None, "section"),
        P("expert", "section", None),
        P(),
    )
    return jax.shard_map(shards, mesh=mesh, in_specs=in_specs, out_specs=out_specs, check_vma=False)
```

profile of v0, /device:TPU:1, one launch (start us, length us, event | category | flops | bytes accessed | tf_op | source)
XLA Modules:
  0.0 798.1 jit_solution(7832499318834523150)
XLA Ops:
  7.2 0.0 all-gather.3.cloned.1.call-start
  7.2 1.8 copy.35
  9.0 0.7 multiply_add_fusion
  9.7 88.7 %all-gather.3.cloned.1.call-done = bf16[192,6144]{0,1:T(8,128)(2,1)} async-done(((bf16[192,192]{0,1:T(8,128)(2,1)}), bf16[192,6144]{0,1:T(8,128)(2,1)}) %all-gather.3.cloned.1.call-update) | async-done | bytes 2359312 | tf_op jit(solution)/shard_map/all_gather | solution.py:37
  98.5 3.4 fusion.39
  101.8 0.7 select_reduce_fusion.1
  102.6 0.5 copy-done.10
  103.2 0.2 select_reduce_fusion
  103.4 3.7 convolution_convert_fusion.2
  107.0 4.7 all-to-all-start
  111.8 0.0 all-gather.5.cloned.1.call-start
  111.8 0.7 copy.37
  112.6 0.0 reduce-scatter.3.cloned.1.call-start
  112.6 53.5 %all-to-all-done = bf16[8,48,6144]{2,1,0:T(8,128)(2,1)} async-done(((bf16[8,48,6144]{2,1,0:T(8,128)(2,1)}), bf16[8,48,6144]{2,1,0:T(8,128)(2,1)}, u32[]{:S(2)}, u32[]{:S(2)}) %all-to-all-start) | async-done | bytes 4718624 | tf_op jit(solution)/shard_map/all_to_all | solution.py:45
  166.2 4.7 fusion.6
  170.9 4.1 convolution_convert_fusion.1
  175.0 0.0 reduce-scatter.5.cloned.1.call-start
  175.1 21.7 %all-gather.5.cloned.1.call-done = bf16[192,6144]{0,1:T(8,128)(2,1)} async-done(((bf16[192,192]{0,1:T(8,128)(2,1)}), bf16[192,6144]{0,1:T(8,128)(2,1)}) %all-gather.5.cloned.1.call-update) | async-done | bytes 2359312 | tf_op jit(solution)/shard_map/all_gather | solution.py:38
  196.7 3.8 multiply_convert_fusion
  200.6 61.3 %all_to_all.20 = bf16[8,48,6144]{2,1,0:T(8,128)(2,1)S(1)} all-to-all(bf16[8,48,6144]{2,1,0:T(8,128)(2,1)S(1)} %bitcast.60), channel_id=1, replica_groups=mesh['section'=32,'expert'=8] {'expert'}, dimensions={0} | all-to-all | bytes 9437184 | tf_op jit(solution)/shard_map/all_to_all | solution.py:48
  261.9 2.1 copy-done.1
  264.0 1.4 fusion.14
  265.4 0.7 copy-done.6
  266.1 4.0 convolution_convert_fusion
  270.2 0.6 fusion.38
  270.8 0.7 fusion.30
  271.4 5.9 fusion
  277.3 49.2 %reduce-scatter.3.cloned.1.call-done = bf16[384,192]{0,1:T(8,128)(2,1)} async-done(((bf16[384,6144]{0,1:T(8,128)(2,1)}), bf16[384,192]{0,1:T(8,128)(2,1)}) %reduce-scatter.3.cloned.1.call-update) | async-done | bytes 147472 | tf_op jit(solution)/shard_map/reduce_scatter | solution.py:74
  326.5 1.7 copy.36
  328.2 4.9 all-to-all-start.1
  333.1 5.9 fusion.1
  338.9 121.7 %reduce-scatter.5.cloned.1.call-done = bf16[384,192]{0,1:T(8,128)(2,1)} async-done(((bf16[384,6144]{0,1:T(8,128)(2,1)}), bf16[384,192]{0,1:T(8,128)(2,1)}) %reduce-scatter.5.cloned.1.call-update) | async-done | bytes 147472 | tf_op jit(solution)/shard_map/reduce_scatter | solution.py:77
  460.6 1.7 copy.38
  462.3 3.8 all-to-all-start.3
  466.2 1.2 fusion.21
  467.4 2.0 fusion.23
  469.4 70.1 %all-reduce = (f32[192]{0:T(256)S(1)}, f32[192]{0:T(256)S(1)}) all-reduce(f32[192]{0:T(256)S(1)} %get-tuple-element.26, f32[192]{0:T(256)S(1)} %get-tuple-element.25), channel_id=1, replica_groups=mesh['section'=32,'expert'=8] {'section'}, use_global_device_ids=true, to_apply=%region_6.0 | all-reduce | flops 384 | bytes 3072 | tf_op jit(solution)/shard_map/psum | solution.py:107
  539.4 0.7 multiply_multiply_fusion
  540.1 0.6 copy-done.8
  540.7 1.7 convolution_bitcast_fusion
  542.3 0.9 dynamic_update_slice.3
  543.3 0.7 copy-done.5
  544.0 1.1 fusion.33
  545.1 0.9 fusion.20
  546.0 1.6 fusion.18
  547.6 1.6 copy.40
  549.2 240.7 %all-reduce.3.cloned.1.call-done = f32[6144,8]{0,1:T(8,128)} async-done(((f32[6144,8]{0,1:T(8,128)}), f32[6144,8]{0,1:T(8,128)}) %all-reduce.3.cloned.1.call-update) | async-done | bytes 196624 | tf_op jit(solution)/shard_map/psum | solution.py:125
  789.9 1.6 copy.43
  (29 shorter events, 0.2 us)
Async XLA Ops:
  7.2 163.7 %copy-start = (bf16[1,256,6144]{2,1,0:T(8,128)(2,1)S(1)}, bf16[1,256,6144]{2,1,0:T(8,128)(2,1)}, u32[]{:S(2)}) copy-start(bf16[1,256,6144]{2,1,0:T(8,128)(2,1)} %param.12) | copy-start | bytes 9437188
  7.2 91.3 %all-gather.3.cloned.1.call-start = ((), (), s32[]{:S(2)}) async-start(), calls=%async_computation.6 | async-start | bytes 3244032 | tf_op jit(solution)/shard_map/all_gather | solution.py:37
  98.5 4.9 copy-start.2
  102.6 0.6 copy-start.10
  102.6 0.6 copy-start.9
  103.3 3.7 copy-start.4
  107.0 4.8 copy-start.7
  107.0 59.1 %all-to-all-start = ((bf16[8,48,6144]{2,1,0:T(8,128)(2,1)}), bf16[8,48,6144]{2,1,0:T(8,128)(2,1)}, u32[]{:S(2)}, u32[]{:S(2)}) async-start(bf16[8,48,6144]{2,1,0:T(8,128)(2,1)} %bitcast.59), calls=%async_computation | async-start | bytes 9437184 | tf_op jit(solution)/shard_map/all_to_all | solution.py:45
  111.8 85.0 %all-gather.5.cloned.1.call-start = ((), (), s32[]{:S(2)}) async-start(), calls=%async_computation.8 | async-start | bytes 3244032 | tf_op jit(solution)/shard_map/all_gather | solution.py:38
  112.6 213.9 %reduce-scatter.3.cloned.1.call-start = ((), (), s32[]{:S(2)}) async-start(), calls=%async_computation.7 | async-start | bytes 4866048 | tf_op jit(solution)/shard_map/reduce_scatter | solution.py:74
  175.0 285.6 %reduce-scatter.5.cloned.1.call-start = ((), (), s32[]{:S(2)}) async-start(), calls=%async_computation.9 | async-start | bytes 4866048 | tf_op jit(solution)/shard_map/reduce_scatter | solution.py:77
  261.9 2.1 copy-start.1
  264.0 2.1 copy-start.3
  265.4 0.7 copy-start.6
  328.2 134.1 %all-to-all-start.1 = ((bf16[8,48,192]{2,1,0:T(8,128)(2,1)}), bf16[8,48,192]{2,1,0:T(8,128)(2,1)}, u32[]{:S(2)}, u32[]{:S(2)}) async-start(bf16[8,48,192]{2,1,0:T(8,128)(2,1)} %bitcast.63), calls=%async_computation.2 | async-start | bytes 393216 | tf_op jit(solution)/shard_map/all_to_all | solution.py:83
  462.3 82.7 %all-to-all-start.3 = ((bf16[8,48,192]{2,1,0:T(8,128)(2,1)}), bf16[8,48,192]{2,1,0:T(8,128)(2,1)S(1)}, u32[]{:S(2)}, u32[]{:S(2)}) async-start(bf16[8,48,192]{2,1,0:T(8,128)(2,1)} %bitcast.12), calls=%async_computation.5 | async-start | bytes 393216 | tf_op jit(solution)/shard_map/all_to_all | solution.py:90
  466.1 323.8 %all-reduce.3.cloned.1.call-start = ((), (), s32[]{:S(2)}) async-start(), calls=%async_computation.10 | async-start | bytes 393216 | tf_op jit(solution)/shard_map/psum | solution.py:125
  540.1 0.6 copy-start.8
  543.3 0.7 copy-start.5
Sparse Core Ops, SparseCore 0:
  11.3 87.0 all-gather.2
  115.9 80.7 all-gather.4
  201.0 125.4 reduce-scatter.2
  330.6 129.9 reduce-scatter.4
  544.1 245.8 all-reduce.2
where the time goes:
time: 799 us; the launch traced here: 798 us
  waiting for transfers between devices  576 us (72%)
  blocking collectives  131 us (16%)
  matrix products  45.3 us (6%)
  local copies, waits for them, and re-layouts  15.4 us (2%)
  between operations  14 us (2%)
  starting transfers between devices  13.5 us (2%)
    psum x1, waiting for transfers between devices, shards(): grad_router = lax.psum(placed_router, ('section', 'expert'))  241 us
    reduce_scatter x1, waiting for transfers between devices, shards(): lax.psum_scatter(backward_part.astype(jnp.bfloat16), 'section', scatter_d...  122 us
    all_gather x1, waiting for transfers between devices, shards(): lax.all_gather(tokens, 'section', axis=1, tiled=True)  88.7 us
    psum x1, blocking collectives, shards(): lax.psum((jnp.sum(cot_float * out_first, axis=1), jnp.sum(cot_float * out...  70.1 us
    all_to_all x1, blocking collectives, shards(): lax.all_to_all(sent_cot.reshape(block_shape), 'expert', split_axis=0, con...  61.3 us
    all_to_all x1, waiting for transfers between devices, shards(): lax.all_to_all(sent_in.reshape(block_shape), 'expert', split_axis=0, conc...  53.5 us
    reduce_scatter x1, waiting for transfers between devices, shards(): lax.psum_scatter(forward_part.astype(jnp.bfloat16), 'section', scatter_di...  49.2 us
    all_gather x1, waiting for transfers between devices, shards(): lax.all_gather(cotangent, 'section', axis=1, tiled=True)  21.7 us
  transfers between devices with their start and end apart: 8, of which 6 were waited for; matrix products, arithmetic and copies ran while one was open for 6% of the time, Pallas kernels for 0%

commit v1 on v0

--- a/solution.py
+++ b/solution.py
@@ -122,7 +122,7 @@
     placed_router = lax.dynamic_update_slice(
         jnp.zeros((model_width, n_expert), jnp.float32), local_router, (feat_start, jnp.int32(0))
     )
-    grad_router = lax.psum(placed_router, ("section", "expert"))
+    grad_router = lax.psum(lax.psum(placed_router, "section"), "expert")
     return (
         mixed.astype(jnp.bfloat16),
         grad_tokens.astype(jnp.bfloat16),

time: 799 us -> 885 us (1.11)
  waiting for transfers between devices: 576 us -> 656 us
    psum x1 -> x2, waiting for transfers between devices: 241 us -> 321 us  [shards(): grad_router = lax.psum(lax.psum(placed_router, 'section'), 'expert')]
  transfers between devices with their start and end apart: 8 -> 9, of which waited for: 6 -> 7; matrix products, arithmetic and copies ran while one was open for 6% -> 6% of each run, Pallas kernels for 0% -> 0%
where the time goes in v1:
time: 885 us; the launch traced here: 880 us
  waiting for transfers between devices  656 us (74%)
  blocking collectives  131 us (15%)
  matrix products  46.3 us (5%)
  local copies, waits for them, and re-layouts  15.4 us (2%)
  starting transfers between devices  14.7 us (2%)
  between operations  14.3 us (2%)
    psum x2, waiting for transfers between devices, shards(): grad_router = lax.psum(lax.psum(placed_router, 'section'), 'expert')  321 us
    reduce_scatter x1, waiting for transfers between devices, shards(): lax.psum_scatter(backward_part.astype(jnp.bfloat16), 'section', scatter_d...  121 us
    all_gather x1, waiting for transfers between devices, shards(): lax.all_gather(tokens, 'section', axis=1, tiled=True)  88.7 us
    psum x1, blocking collectives, shards(): lax.psum((jnp.sum(cot_float * out_first, axis=1), jnp.sum(cot_float * out...  69.8 us
    all_to_all x1, blocking collectives, shards(): lax.all_to_all(sent_cot.reshape(block_shape), 'expert', split_axis=0, con...  61.3 us
    all_to_all x1, waiting for transfers between devices, shards(): lax.all_to_all(sent_in.reshape(block_shape), 'expert', split_axis=0, conc...  53.5 us
    reduce_scatter x1, waiting for transfers between devices, shards(): lax.psum_scatter(forward_part.astype(jnp.bfloat16), 'section', scatter_di...  49.2 us
    all_gather x1, waiting for transfers between devices, shards(): lax.all_gather(cotangent, 'section', axis=1, tiled=True)  21.7 us
  transfers between devices with their start and end apart: 9, of which 7 were waited for; matrix products, arithmetic and copies ran while one was open for 6% of the time, Pallas kernels for 0%

profile of v1, /device:TPU:1, one launch (start us, length us, event | category | flops | bytes accessed | tf_op | source)
XLA Modules:
  0.0 880.2 jit_solution(13923411438757634607)
XLA Ops:
  7.2 1.8 copy.35
  9.0 0.7 multiply_add_fusion
  9.7 88.7 %all-gather.3.cloned.1.call-done = bf16[192,6144]{0,1:T(8,128)(2,1)} async-done(((bf16[192,192]{0,1:T(8,128)(2,1)}), bf16[192,6144]{0,1:T(8,128)(2,1)}) %all-gather.3.cloned.1.call-update) | async-done | bytes 2359312 | tf_op jit(solution)/shard_map/all_gather | solution.py:37
  98.5 3.4 fusion.39
  101.8 0.7 select_reduce_fusion.1
  102.6 0.5 copy-done.10
  103.1 0.0 copy-done.9
  103.2 0.2 select_reduce_fusion
  103.4 3.7 convolution_convert_fusion.2
  107.0 4.7 all-to-all-start
  111.8 0.0 all-gather.5.cloned.1.call-start
  111.8 0.7 copy.37
  112.6 0.0 reduce-scatter.3.cloned.1.call-start
  112.6 53.5 %all-to-all-done = bf16[8,48,6144]{2,1,0:T(8,128)(2,1)} async-done(((bf16[8,48,6144]{2,1,0:T(8,128)(2,1)}), bf16[8,48,6144]{2,1,0:T(8,128)(2,1)}, u32[]{:S(2)}, u32[]{:S(2)}) %all-to-all-start) | async-done | bytes 4718624 | tf_op jit(solution)/shard_map/all_to_all | solution.py:45
  166.2 4.7 fusion.6
  170.9 4.1 convolution_convert_fusion.1
  175.1 21.7 %all-gather.5.cloned.1.call-done = bf16[192,6144]{0,1:T(8,128)(2,1)} async-done(((bf16[192,192]{0,1:T(8,128)(2,1)}), bf16[192,6144]{0,1:T(8,128)(2,1)}) %all-gather.5.cloned.1.call-update) | async-done | bytes 2359312 | tf_op jit(solution)/shard_map/all_gather | solution.py:38
  196.7 3.8 multiply_convert_fusion
  200.6 61.3 %all_to_all.20 = bf16[8,48,6144]{2,1,0:T(8,128)(2,1)S(1)} all-to-all(bf16[8,48,6144]{2,1,0:T(8,128)(2,1)S(1)} %bitcast.60), channel_id=1, replica_groups=mesh['section'=32,'expert'=8] {'expert'}, dimensions={0} | all-to-all | bytes 9437184 | tf_op jit(solution)/shard_map/all_to_all | solution.py:48
  261.9 2.1 copy-done.1
  264.0 1.4 fusion.14
  265.4 0.7 copy-done.6
  266.1 4.0 convolution_convert_fusion
  270.2 0.6 fusion.38
  270.7 0.7 fusion.30
  271.4 5.9 fusion
  277.3 49.2 %reduce-scatter.3.cloned.1.call-done = bf16[384,192]{0,1:T(8,128)(2,1)} async-done(((bf16[384,6144]{0,1:T(8,128)(2,1)}), bf16[384,192]{0,1:T(8,128)(2,1)}) %reduce-scatter.3.cloned.1.call-update) | async-done | bytes 147472 | tf_op jit(solution)/shard_map/reduce_scatter | solution.py:74
  326.5 1.7 copy.36
  328.3 4.8 all-to-all-start.1
  333.1 5.9 fusion.1
  339.0 120.9 %reduce-scatter.5.cloned.1.call-done = bf16[384,192]{0,1:T(8,128)(2,1)} async-done(((bf16[384,6144]{0,1:T(8,128)(2,1)}), bf16[384,192]{0,1:T(8,128)(2,1)}) %reduce-scatter.5.cloned.1.call-update) | async-done | bytes 147472 | tf_op jit(solution)/shard_map/reduce_scatter | solution.py:77
  459.8 1.7 copy.38
  461.5 4.8 all-to-all-start.3
  466.4 1.2 fusion.21
  467.7 2.0 fusion.23
  469.7 69.8 %all-reduce = (f32[192]{0:T(256)S(1)}, f32[192]{0:T(256)S(1)}) all-reduce(f32[192]{0:T(256)S(1)} %get-tuple-element.26, f32[192]{0:T(256)S(1)} %get-tuple-element.25), channel_id=1, replica_groups=mesh['section'=32,'expert'=8] {'section'}, use_global_device_ids=true, to_apply=%region_6.0 | all-reduce | flops 384 | bytes 3072 | tf_op jit(solution)/shard_map/psum | solution.py:107
  539.4 0.7 multiply_multiply_fusion
  540.1 0.6 copy-done.8
  540.7 1.7 convolution_bitcast_fusion
  542.4 0.9 dynamic_update_slice.3
  543.3 0.7 copy-done.5
  544.1 1.6 copy.40
  545.7 0.9 fusion.20
  546.6 1.8 fusion.33
  548.4 248.2 %all-reduce.4.cloned.1.call-done = f32[6144,8]{0,1:T(8,128)} async-done(((f32[6144,8]{0,1:T(8,128)}), f32[6144,8]{0,1:T(8,128)}) %all-reduce.4.cloned.1.call-update) | async-done | bytes 196624 | tf_op jit(solution)/shard_map/psum | solution.py:125
  796.7 1.8 fusion.18
  798.5 73.2 %all-reduce.6.cloned.1.call-done = f32[6144,8]{0,1:T(8,128)} async-done(((f32[6144,8]{0,1:T(8,128)}), f32[6144,8]{0,1:T(8,128)}) %all-reduce.6.cloned.1.call-update) | async-done | bytes 196624 | tf_op jit(solution)/shard_map/psum | solution.py:125
  871.7 1.6 copy.44
  (32 shorter events, 0.3 us)
Async XLA Ops:
  7.2 163.8 %copy-start = (bf16[1,256,6144]{2,1,0:T(8,128)(2,1)S(1)}, bf16[1,256,6144]{2,1,0:T(8,128)(2,1)}, u32[]{:S(2)}) copy-start(bf16[1,256,6144]{2,1,0:T(8,128)(2,1)} %param.12) | copy-start | bytes 9437188
  7.2 91.3 %all-gather.3.cloned.1.call-start = ((), (), s32[]{:S(2)}) async-start(), calls=%async_computation.6 | async-start | bytes 3244032 | tf_op jit(solution)/shard_map/all_gather | solution.py:37
  98.5 4.9 copy-start.2
  102.6 0.5 copy-start.10
  102.6 0.6 copy-start.9
  103.3 3.7 copy-start.4
  107.0 4.8 copy-start.7
  107.0 59.1 %all-to-all-start = ((bf16[8,48,6144]{2,1,0:T(8,128)(2,1)}), bf16[8,48,6144]{2,1,0:T(8,128)(2,1)}, u32[]{:S(2)}, u32[]{:S(2)}) async-start(bf16[8,48,6144]{2,1,0:T(8,128)(2,1)} %bitcast.59), calls=%async_computation | async-start | bytes 9437184 | tf_op jit(solution)/shard_map/all_to_all | solution.py:45
  111.8 85.0 %all-gather.5.cloned.1.call-start = ((), (), s32[]{:S(2)}) async-start(), calls=%async_computation.8 | async-start | bytes 3244032 | tf_op jit(solution)/shard_map/all_gather | solution.py:38
  112.6 213.9 %reduce-scatter.3.cloned.1.call-start = ((), (), s32[]{:S(2)}) async-start(), calls=%async_computation.7 | async-start | bytes 4866048 | tf_op jit(solution)/shard_map/reduce_scatter | solution.py:74
  175.0 284.8 %reduce-scatter.5.cloned.1.call-start = ((), (), s32[]{:S(2)}) async-start(), calls=%async_computation.9 | async-start | bytes 4866048 | tf_op jit(solution)/shard_map/reduce_scatter | solution.py:77
  261.9 2.1 copy-start.1
  264.0 2.1 copy-start.3
  265.4 0.7 copy-start.6
  328.3 133.3 %all-to-all-start.1 = ((bf16[8,48,192]{2,1,0:T(8,128)(2,1)}), bf16[8,48,192]{2,1,0:T(8,128)(2,1)}, u32[]{:S(2)}, u32[]{:S(2)}) async-start(bf16[8,48,192]{2,1,0:T(8,128)(2,1)} %bitcast.63), calls=%async_computation.2 | async-start | bytes 393216 | tf_op jit(solution)/shard_map/all_to_all | solution.py:83
  461.5 84.2 %all-to-all-start.3 = ((bf16[8,48,192]{2,1,0:T(8,128)(2,1)}), bf16[8,48,192]{2,1,0:T(8,128)(2,1)S(1)}, u32[]{:S(2)}, u32[]{:S(2)}) async-start(bf16[8,48,192]{2,1,0:T(8,128)(2,1)} %bitcast.12), calls=%async_computation.5 | async-start | bytes 393216 | tf_op jit(solution)/shard_map/all_to_all | solution.py:90
  466.4 330.2 %all-reduce.4.cloned.1.call-start = ((), (), s32[]{:S(2)}) async-start(), calls=%async_computation.10 | async-start | bytes 393216 | tf_op jit(solution)/shard_map/psum | solution.py:125
  540.1 0.6 copy-start.8
  543.3 0.7 copy-start.5
  544.0 327.7 %all-reduce.6.cloned.1.call-start = ((), (), s32[]{:S(2)}) async-start(), calls=%async_computation.11 | async-start | bytes 393216 | tf_op jit(solution)/shard_map/psum | solution.py:125
Sparse Core Ops, SparseCore 0:
  11.3 87.0 all-gather.2
  115.9 80.7 all-gather.4
  201.0 125.5 reduce-scatter.2
  330.6 129.1 reduce-scatter.4
  544.1 252.4 all-reduce.3
  799.1 72.5 all-reduce.5
